TPU v7x, 32 devices: a whole 2x2x4 slice. The times are simulated.
32 devices in a mesh: groups: 2 (over x), out: 16 (over z, y, core).
Axes of the slice: x: 2, y: 2, z: 4, core: 2. Of those that a mesh axis runs over, the one named last changes fastest.
Arguments:
- tokens: bfloat16 [256, 8192], P('groups', 'out'), parts along dimension 0, may hold values from -60 to 60, as said below
- grad_hidden: bfloat16 [256, 16384], P('groups', 'out'), parts along dimension 0, may hold values from -6 to 6
- w_gate: bfloat16 [8192, 16384], P(None, 'out'), may hold values from -0.0625 to 0.0625
- w_up: bfloat16 [8192, 16384], P(None, 'out'), may hold values from -0.0625 to 0.0625
- a_factors: bfloat16 [8192, 128], replicated, may hold values from -0.0625 to 0.0625
- b_factors: bfloat16 [2, 64, 16384], P(None, None, 'out'), may hold values from -0.75 to 0.75
- magnitudes: float32 [2, 16384], P(None, 'out'), may hold values from 1 to 2
Outputs:
- hidden: bfloat16 [256, 16384], P('groups', 'out'), parts along dimension 0
- grad_tokens: bfloat16 [256, 8192], P('groups', 'out'), parts along dimension 0
- step_a: float32 [16384, 128], P(('groups', 'out')), parts along dimension 0
- step_b: float32 [4, 64, 16384], P('groups', None, 'out'), parts along dimension 0
- step_m: float32 [4, 16384], P('groups', 'out'), parts along dimension 0
There are 2 independent parts, one for each index of `groups`. A program takes and returns all parts, laid end to end along the dimension named above; an argument that names none is the same for every part. Nothing has to cross between parts.
Inputs may be any that keep to these rules, and one draw needn't show every extreme that they name: `tokens`: activations with feature scales that differ between features.
All inputs are finite; a program needn't handle non-finite values.
Results may differ from a plain program's by a relative error of at most 0.0073.
Values may be sent and summed in bfloat16 or wider, within the bound.
A program may use at most 128 MiB of HBM per device.

v0:
```python
import jax
import jax.numpy as jnp
from jax import lax
from jax.sharding import PartitionSpec as P

D = 8192
FW = 16384
R = 64


def inner_product(left_side, right_side, precision=None):
    return lax.dot_general(
        left_side,
        right_side,
        (((0,), (0,)), ((), ())),
        precision=precision,
        preferred_element_type=jnp.float32,
    )


def outer_contract(left_side, right_side, precision=None):
    return lax.dot_general(
        left_side,
        right_side,
        (((1,), (1,)), ((), ())),
        precision=precision,
        preferred_element_type=jnp.float32,
    )


def split_parts(values):
    upper = values.astype(jnp.bfloat16)
    lower = (values - upper.astype(jnp.float32)).astype(jnp.bfloat16)
    return (upper, lower)


def per_device(tokens, grad_hidden, w_gate, w_up, a_factors, b_factors, magnitudes):
    weights = (w_gate, w_up)
    rank = a_factors.shape[1] // 2
    count_tokens = tokens.shape[0]
    norms = []
    scales = []
    for which in range(2):
        weight = weights[which]
        left = a_factors[:, which * rank : (which + 1) * rank]
        right = b_factors[which]
        merged = weight.astype(jnp.float32) + jnp.dot(
            left, right, preferred_element_type=jnp.float32
        )
        squares = jnp.sum(merged * merged, axis=0)
        norm_col = jnp.sqrt(squares + 1e-06)
        norms.append(norm_col)
        scales.append(magnitudes[which] / norm_col)
    whole = lax.all_gather(tokens, "out", axis=1, tiled=True)
    base_gate = jnp.dot(whole, w_gate, preferred_element_type=jnp.float32)
    base_up = jnp.dot(whole, w_up, preferred_element_type=jnp.float32)
    low_wide = jnp.dot(whole, a_factors, preferred_element_type=jnp.float32)
    low = low_wide.astype(jnp.bfloat16)
    bases = []
    pres = []
    for which, raw in enumerate((base_gate, base_up)):
        base = raw + jnp.dot(
            low[:, which * rank : (which + 1) * rank],
            b_factors[which],
            preferred_element_type=jnp.float32,
        )
        bases.append(base)
        pres.append(base * scales[which][None, :])
    sigma = jax.nn.sigmoid(pres[0])
    hidden = (pres[0] * sigma * pres[1]).astype(jnp.bfloat16)
    cotangent = grad_hidden.astype(jnp.float32)
    dpres = (
        cotangent * pres[1] * sigma * (1.0 + pres[0] * (1.0 - sigma)),
        cotangent * pres[0] * sigma,
    )
    partial_sum = jnp.zeros((count_tokens, w_gate.shape[0]), jnp.float32)
    z_blocks = []
    grad_bs = []
    grad_ms = []
    for which in range(2):
        dscaled = (dpres[which] * scales[which][None, :]).astype(jnp.bfloat16)
        grad_ms.append(jnp.sum(dpres[which] * bases[which], axis=0) / norms[which])
        grad_bs.append(inner_product(low[:, which * rank : (which + 1) * rank], dscaled))
        z_blocks.append(outer_contract(dscaled, b_factors[which]))
        partial_sum = partial_sum + outer_contract(dscaled, weights[which])
    z_local = jnp.concatenate(z_blocks, axis=1)
    grad_b = jnp.stack(grad_bs)
    grad_m = jnp.stack(grad_ms)
    summed_inputs = lax.psum_scatter(partial_sum, "out", scatter_dimension=1, tiled=True)
    local_energy = jnp.sum(grad_b * grad_b) + jnp.sum(grad_m * grad_m)
    z_all, small_energy = lax.psum((z_local, local_energy), "out")
    z_upper, z_lower = split_parts(z_all)
    full_a = inner_product(whole, z_upper) + inner_product(whole, z_lower)
    grad_a = inner_product(tokens, z_upper) + inner_product(tokens, z_lower)
    mine = tokens.shape[1]
    a_mine = lax.dynamic_slice_in_dim(a_factors, lax.axis_index("out") * mine, mine, 0)
    adapter = outer_contract(z_upper, a_mine) + outer_contract(z_lower, a_mine)
    grad_tokens = (summed_inputs + adapter).astype(jnp.bfloat16)
    energy = small_energy + jnp.sum(full_a * full_a)
    count_all = 2 * D * R + 2 * R * FW + 2 * FW
    rms_value = jnp.sqrt(energy / count_all + 1e-06)
    return (hidden, grad_tokens, grad_a / rms_value, grad_b / rms_value, grad_m / rms_value)


def solution(mesh):
    in_specs = (
        P("groups", "out"),
        P("groups", "out"),
        P(None, "out"),
        P(None, "out"),
        P(),
        P(None, None, "out"),
        P(None, "out"),
    )
    out_specs = (
        P("groups", "out"),
        P("groups", "out"),
        P(("groups", "out"), None),
        P("groups", None, "out"),
        P("groups", "out"),
    )
    return jax.shard_map(
        per_device, mesh=mesh, in_specs=in_specs, out_specs=out_specs, check_vma=False
    )
```

profile of v0, /device:TPU:0, one launch (start us, length us, event | category | flops | bytes accessed | tf_op | source)
XLA Modules:
  0.0 256.2 jit_solution(1929650667966069490)
XLA Ops:
  7.2 0.0 all-gather.2.cloned.1.call-start
  7.2 0.7 all-gather.2.cloned.1.call-update
  7.9 0.0 copy-start.2
  7.9 0.0 copy-start.3
  7.9 0.0 all-reduce.2.cloned.1.call-start
  8.0 0.0 copy-start
  8.0 8.9 %multiply_reduce_fusion.1 = f32[1024]{0:T(1024)S(1)} fusion(bf16[8192,1024]{1,0:T(8,128)(2,1)} %param.9, bf16[8192,128]{1,0:T(8,128)(2,1)} %param.11, bf16[2,64,1024]{2,1,0:T(8,128)(2,1)} %param.12), kind=kOutput, calls=%fused_computation.1 | convolution fusion | flops 1107295232 | bytes 19009536 | tf_op jit(solution)/shard_map/dot_general | solution.py:47
  16.9 0.0 copy-done.2
  16.9 0.0 copy-done.3
  16.9 2.9 %copy-done = bf16[8192,1024]{1,0:T(8,128)(2,1)S(1)} copy-done((bf16[8192,1024]{1,0:T(8,128)(2,1)S(1)}, bf16[8192,1024]{1,0:T(8,128)(2,1)}, u32[]{:S(2)}) %copy-start) | copy-done | bytes 16777240
  19.8 0.0 copy-start.5
  19.8 5.5 %multiply_reduce_fusion = f32[1024]{0:T(1024)S(1)} fusion(bf16[8192,1024]{1,0:T(8,128)(2,1)S(1)} %copy-done, bf16[8192,128]{1,0:T(8,128)(2,1)S(1)} %copy-done.2, bf16[2,64,1024]{2,1,0:T(8,128)(2,1)S(1)} %copy-done.3), kind=kOutput, calls=%fused_computation | convolution fusion | flops 1107295232 | bytes 19009536 | tf_op jit(solution)/shard_map/dot_general | solution.py:47
  25.4 0.0 copy-done.5
  25.4 28.7 %all-gather.2.cloned.1.call-done = bf16[128,8192]{1,0:T(8,128)(2,1)} async-done(((bf16[128,512]{1,0:T(8,128)(2,1)}), bf16[128,8192]{1,0:T(8,128)(2,1)}) %all-gather.2.cloned.1.call-update) | async-done | bytes 2097168 | tf_op jit(solution)/shard_map/all_gather | solution.py:54
  54.1 0.0 slice-start
  54.1 2.7 %convolution_convert_fusion = bf16[128,128]{0,1:T(8,128)(2,1)S(1)} fusion(bf16[128,8192]{1,0:T(8,128)(2,1)} %all-gather.2.cloned.1.call-done, bf16[8192,128]{1,0:T(8,128)(2,1)S(1)} %copy-done.2), kind=kOutput, calls=%fused_computation.18 | convolution fusion | flops 268451840 | bytes 4227072 | tf_op jit(solution)/shard_map/dot_general | solution.py:57
  56.8 0.0 slice-start.1
  56.8 0.0 slice-start.2
  56.8 0.0 slice-start.3
  56.8 0.0 copy-start.1
  56.8 8.9 %fusion.36 = f32[128,1024]{1,0:T(8,128)S(1)} fusion(bf16[128,8192]{1,0:T(8,128)(2,1)} %all-gather.2.cloned.1.call-done, bf16[8192,1024]{1,0:T(8,128)(2,1)} %param.10), kind=kOutput, calls=%fused_computation.66 | convolution fusion | flops 2147483648 | bytes 19398656 | tf_op jit(solution)/shard_map/dot_general | solution.py:56
  65.7 0.3 convolution_add_fusion.2
  65.9 0.0 slice-done
  66.0 0.0 slice-done.1
  66.0 0.0 slice-done.2
  66.0 0.8 slice-done.3
  66.8 0.6 copy-done.1
  67.4 0.0 copy-start.6
  67.4 2.5 fusion.35
  69.9 0.0 copy-done.6
  69.9 1.3 multiply_reduce_fusion.3
  71.2 0.2 fusion.16
  71.4 13.2 %fusion.37 = f32[128,8192]{1,0:T(8,128)} fusion(bf16[128,1024]{1,0:T(8,128)(2,1)S(1)} %get-tuple-element.14, bf16[8192,1024]{1,0:T(8,128)(2,1)} %param.9), kind=kOutput, calls=%fused_computation.67 | convolution fusion | flops 2147483648 | bytes 21233664 | tf_op jit(solution)/shard_map/dot_general | solution.py:22
  84.7 0.2 fusion.12
  84.9 0.6 pad_maximum_fusion.1
  85.5 0.0 all-reduce.2.cloned.1.call-update
  85.6 0.3 reduce-scatter.2.cloned.1.call-start
  85.8 14.5 %convolution_add_fusion.1 = f32[128,8192]{1,0:T(8,128)} fusion(f32[128,8192]{1,0:T(8,128)} %fusion.37, bf16[128,1024]{1,0:T(8,128)(2,1)S(1)} %get-tuple-element.16, bf16[8192,1024]{1,0:T(8,128)(2,1)} %param.10), kind=kOutput, calls=%fused_computation.4 | convolution fusion | flops 2148532224 | bytes 25427968 | tf_op jit(solution)/shard_map/dot_general | solution.py:22
  100.4 0.0 reduce-scatter.2.cloned.1.call-update
  100.4 0.6 multiply_reduce_fusion.5
  101.0 0.2 convolution_bitcast_fusion
  101.2 0.2 convolution_bitcast_fusion.1
  101.4 0.7 multiply_reduce_fusion.4
  103.4 32.1 %psum.15 = f32[]{:T(128)} all-reduce(f32[]{:T(128)S(6)} %add.96), channel_id=1, replica_groups=mesh['groups'=2,'out'=16] {'out'}, use_global_device_ids=true, to_apply=%region_8.0 | all-reduce | flops 1 | bytes 8 | tf_op jit(solution)/shard_map/psum | solution.py:91
  135.5 33.7 %all-reduce.2.cloned.1.call-done = f32[128,128]{0,1:T(8,128)} async-done(((f32[128,128]{0,1:T(8,128)}), f32[128,128]{0,1:T(8,128)}) %all-reduce.2.cloned.1.call-update) | async-done | bytes 65552 | tf_op jit(solution)/shard_map/psum | solution.py:91
  169.2 0.9 subtract_convert_fusion
  170.1 0.7 fusion.39
  170.8 0.0 copy-start.4
  170.8 1.9 fusion.3
  174.1 0.0 copy-done.4
  174.1 0.2 fusion.38
  174.3 0.2 fusion.5
  174.5 0.8 copy.12
  175.3 0.6 broadcast_divide_fusion
  175.9 0.9 fusion.11
  176.8 1.1 fusion.21
  177.9 69.9 %reduce-scatter.2.cloned.1.call-done = f32[128,512]{1,0:T(8,128)} async-done(((f32[128,8192]{1,0:T(8,128)}), f32[128,512]{1,0:T(8,128)}) %reduce-scatter.2.cloned.1.call-update) | async-done | bytes 262160 | tf_op jit(solution)/shard_map/reduce_scatter | solution.py:89
  247.8 1.9 fusion.7
  (6 shorter events, 0.0 us)
Async XLA Ops:
  7.2 46.9 %all-gather.2.cloned.1.call-start = ((), (), s32[]{:S(2)}) async-start(), calls=%async_computation.1 | async-start | bytes 2228224 | tf_op jit(solution)/shard_map/all_gather | solution.py:54
  7.9 9.0 %copy-start.2 = (bf16[8192,128]{1,0:T(8,128)(2,1)S(1)}, bf16[8192,128]{1,0:T(8,128)(2,1)}, u32[]{:S(2)}) copy-start(bf16[8192,128]{1,0:T(8,128)(2,1)} %param.11) | copy-start | bytes 6291460
  7.9 9.0 %copy-start.3 = (bf16[2,64,1024]{2,1,0:T(8,128)(2,1)S(1)}, bf16[2,64,1024]{2,1,0:T(8,128)(2,1)}, u32[]{:S(2)}) copy-start(bf16[2,64,1024]{2,1,0:T(8,128)(2,1)} %param.12) | copy-start | bytes 786436
  7.9 161.3 %all-reduce.2.cloned.1.call-start = ((), (), s32[]{:S(2)}) async-start(), calls=%async_computation.3 | async-start | bytes 131072 | tf_op jit(solution)/shard_map/psum | solution.py:91
  8.0 11.9 %copy-start = (bf16[8192,1024]{1,0:T(8,128)(2,1)S(1)}, bf16[8192,1024]{1,0:T(8,128)(2,1)}, u32[]{:S(2)}) copy-start(bf16[8192,1024]{1,0:T(8,128)(2,1)} %param.10) | copy-start | bytes 50331652
  19.8 5.5 %copy-start.5 = (f32[2,1024]{1,0:T(2,128)S(1)}, f32[2,1024]{1,0:T(2,128)}, u32[]{:S(2)}) copy-start(f32[2,1024]{1,0:T(2,128)} %param.13) | copy-start | bytes 24580
  54.1 11.9 %slice-start = ((s8[16777216]{0:T(1024)(128)(4,1)}), s8[4194304]{0:T(1024)(128)(4,1)S(1)}, s32[]{:S(2)}) async-start(s8[16777216]{0:T(1024)(128)(4,1)} %bitcast.52), calls=%async_computation.4 | async-start | bytes 8388608
  56.8 9.2 %slice-start.1 = ((s8[16777216]{0:T(1024)(128)(4,1)}), s8[4194304]{0:T(1024)(128)(4,1)S(1)}, s32[]{:S(2)}) async-start(s8[16777216]{0:T(1024)(128)(4,1)} %bitcast.52), calls=%async_computation.5 | async-start | bytes 8388608
  56.8 9.2 %slice-start.2 = ((s8[16777216]{0:T(1024)(128)(4,1)}), s8[4194304]{0:T(1024)(128)(4,1)S(1)}, s32[]{:S(2)}) async-start(s8[16777216]{0:T(1024)(128)(4,1)} %bitcast.52), calls=%async_computation.6 | async-start | bytes 8388608
  56.8 10.0 %slice-start.3 = ((s8[16777216]{0:T(1024)(128)(4,1)}), s8[4194304]{0:T(1024)(128)(4,1)S(1)}, s32[]{:S(2)}) async-start(s8[16777216]{0:T(1024)(128)(4,1)} %bitcast.52), calls=%async_computation.7 | async-start | bytes 8388608
  56.8 10.6 %copy-start.1 = (bf16[128,8192]{1,0:T(8,128)(2,1)S(1)}, bf16[128,8192]{1,0:T(8,128)(2,1)}, u32[]{:S(2)}) copy-start(bf16[128,8192]{1,0:T(8,128)(2,1)} %all-gather.2.cloned.1.call-done) | copy-start | bytes 6291460
  67.4 2.5 copy-start.6
  85.6 162.2 %reduce-scatter.2.cloned.1.call-start = ((), (), s32[]{:S(2)}) async-start(), calls=%async_computation.2 | async-start | bytes 4456448 | tf_op jit(solution)/shard_map/reduce_scatter | solution.py:89
  170.8 3.3 %copy-start.4 = (bf16[128,512]{1,0:T(8,128)(2,1)S(1)}, bf16[128,512]{1,0:T(8,128)(2,1)}, u32[]{:S(2)}) copy-start(bf16[128,512]{1,0:T(8,128)(2,1)} %param.7) | copy-start | bytes 393220
Sparse Core Ops, SparseCore 0:
  10.2 43.8 all-gather.1
  85.7 83.4 all-reduce.1
  173.6 74.2 reduce-scatter.1
where the time goes:
time: 257 us; the launch traced here: 256 us
  waiting for transfers between devices  133 us (52%)
  matrix products  64.5 us (25%)
  blocking collectives  32.1 us (12%)
  between operations  16.7 us (6%)
  local copies, waits for them, and re-layouts  5.16 us (2%)
  other arithmetic  4.41 us (2%)
    reduce_scatter x1, waiting for transfers between devices, per_device(): lax.psum_scatter(partial_sum, 'out', scatter_dimension=1, tiled=True)  69.9 us
    psum x1, waiting for transfers between devices, per_device(): z_all, small_energy = lax.psum((z_local, local_energy), 'out')  33.7 us
    psum x1, blocking collectives, per_device(): z_all, small_energy = lax.psum((z_local, local_energy), 'out')  32.1 us
    dot_general x6, matrix products, outer_contract(): lax.dot_general(left_side, right_side, (((1,), (1,)), ((), ())), precisio...  31.2 us
    all_gather x1, waiting for transfers between devices, per_device(): whole = lax.all_gather(tokens, 'out', axis=1, tiled=True)  28.7 us
    dot_general x2, matrix products, per_device(): jnp.dot(left, right, preferred_element_type=jnp.float32)  14.4 us
    dot_general x1, matrix products, per_device(): base_up = jnp.dot(whole, w_up, preferred_element_type=jnp.float32)  8.88 us
    unnamed x23, local copies, waits for them, and re-layouts  5.16 us
  transfers between devices with their start and end apart: 3, of which 3 were waited for; matrix products, arithmetic and copies ran while one was open for 15% of the time, Pallas kernels for 0%

commit v1 on v0

--- a/solution.py
+++ b/solution.py
@@ -51,7 +51,16 @@
         norm_col = jnp.sqrt(squares + 1e-06)
         norms.append(norm_col)
         scales.append(magnitudes[which] / norm_col)
-    whole = lax.all_gather(tokens, "out", axis=1, tiled=True)
+    world = lax.axis_size("out")
+    clean = sorted(((k0, (k0 + 1) % world) for k0 in range(world)))
+    u1 = tokens
+    kept_rows = [u1]
+    for q in [*range(1, world)]:
+        u1 = lax.ppermute(u1, "out", clean)
+        kept_rows.insert(0, u1)
+    whole = jnp.roll(
+        jnp.concatenate(kept_rows, axis=1), (lax.axis_index("out") + 1) * tokens.shape[1], axis=1
+    )
     base_gate = jnp.dot(whole, w_gate, preferred_element_type=jnp.float32)
     base_up = jnp.dot(whole, w_up, preferred_element_type=jnp.float32)
     low_wide = jnp.dot(whole, a_factors, preferred_element_type=jnp.float32)

time: 257 us -> 336 us (1.31)
  waiting for transfers between devices: 133 us -> 198 us
  local copies, waits for them, and re-layouts: 5.16 us -> 20 us
    ppermute x0 -> x15, waiting for transfers between devices: none -> 95.1 us  [per_device(): u1 = lax.ppermute(u1, 'out', clean)]
    all_gather x1 -> x0, waiting for transfers between devices: 28.7 us -> none  [per_device(): whole = lax.all_gather(tokens, 'out', axis=1, tiled=True)]
    unnamed x23 -> x88, local copies, waits for them, and re-layouts: 5.16 us -> 20 us
  transfers between devices with their start and end apart: 3 -> 17, of which waited for: 3 -> 16; matrix products, arithmetic and copies ran while one was open for 15% -> 12% of each run, Pallas kernels for 0% -> 0%
where the time goes in v1:
time: 336 us; the launch traced here: 335 us
  waiting for transfers between devices  198 us (59%)
  matrix products  64.1 us (19%)
  blocking collectives  30 us (9%)
  local copies, waits for them, and re-layouts  20 us (6%)
  between operations  17.3 us (5%)
  other arithmetic  4.41 us (1%)
    ppermute x15, waiting for transfers between devices, per_device(): u1 = lax.ppermute(u1, 'out', clean)  95.1 us
    reduce_scatter x1, waiting for transfers between devices, per_device(): lax.psum_scatter(partial_sum, 'out', scatter_dimension=1, tiled=True)  68.8 us
    psum x1, waiting for transfers between devices, per_device(): z_all, small_energy = lax.psum((z_local, local_energy), 'out')  34.4 us
    dot_general x6, matrix products, outer_contract(): lax.dot_general(left_side, right_side, (((1,), (1,)), ((), ())), precisio...  30.4 us
    psum x1, blocking collectives, per_device(): z_all, small_energy = lax.psum((z_local, local_energy), 'out')  30 us
    unnamed x88, local copies, waits for them, and re-layouts  20 us
    dot_general x2, matrix products, per_device(): jnp.dot(left, right, preferred_element_type=jnp.float32)  14.2 us
    dot_general x1, matrix products, per_device(): base_up = jnp.dot(whole, w_up, preferred_element_type=jnp.float32)  9.36 us
  transfers between devices with their start and end apart: 17, of which 16 were waited for; matrix products, arithmetic and copies ran while one was open for 12% of the time, Pallas kernels for 0%

profile of v1, /device:TPU:0, one launch (start us, length us, event | category | flops | bytes accessed | tf_op | source)
XLA Modules:
  0.0 335.0 jit_solution(2590636093917602862)
XLA Ops:
  7.2 0.5 collective-permute-start
  7.7 7.9 %collective-permute-done = bf16[128,512]{1,0:T(8,128)(2,1)S(1)} collective-permute-done((bf16[128,512]{1,0:T(8,128)(2,1)}, bf16[128,512]{1,0:T(8,128)(2,1)S(1)}, u32[]{:S(2)}, u32[]{:S(2)}) %collective-permute-start) | collective-permute-done | bytes 131104 | tf_op jit(solution)/shard_map/ppermute | solution.py:59
  15.6 7.1 %collective-permute-done.1 = bf16[128,512]{1,0:T(8,128)(2,1)S(1)} collective-permute-done((bf16[128,512]{1,0:T(8,128)(2,1)S(1)}, bf16[128,512]{1,0:T(8,128)(2,1)S(1)}, u32[]{:S(2)}, u32[]{:S(2)}) %collective-permute-start.1) | collective-permute-done | bytes 131104 | tf_op jit(solution)/shard_map/ppermute | solution.py:59
  22.7 7.1 %collective-permute-done.2 = bf16[128,512]{1,0:T(8,128)(2,1)S(1)} collective-permute-done((bf16[128,512]{1,0:T(8,128)(2,1)S(1)}, bf16[128,512]{1,0:T(8,128)(2,1)S(1)}, u32[]{:S(2)}, u32[]{:S(2)}) %collective-permute-start.2) | collective-permute-done | bytes 131104 | tf_op jit(solution)/shard_map/ppermute | solution.py:59
  29.8 0.6 copy-done.8
  30.4 7.1 %collective-permute-done.3 = bf16[128,512]{1,0:T(8,128)(2,1)S(1)} collective-permute-done((bf16[128,512]{1,0:T(8,128)(2,1)S(1)}, bf16[128,512]{1,0:T(8,128)(2,1)S(1)}, u32[]{:S(2)}, u32[]{:S(2)}) %collective-permute-start.3) | collective-permute-done | bytes 131104 | tf_op jit(solution)/shard_map/ppermute | solution.py:59
  37.5 0.6 copy-done.10
  38.2 7.1 %collective-permute-done.4 = bf16[128,512]{1,0:T(8,128)(2,1)S(1)} collective-permute-done((bf16[128,512]{1,0:T(8,128)(2,1)S(1)}, bf16[128,512]{1,0:T(8,128)(2,1)S(1)}, u32[]{:S(2)}, u32[]{:S(2)}) %collective-permute-start.4) | collective-permute-done | bytes 131104 | tf_op jit(solution)/shard_map/ppermute | solution.py:59
  45.3 0.6 copy-done.12
  45.9 7.1 %collective-permute-done.5 = bf16[128,512]{1,0:T(8,128)(2,1)S(1)} collective-permute-done((bf16[128,512]{1,0:T(8,128)(2,1)S(1)}, bf16[128,512]{1,0:T(8,128)(2,1)S(1)}, u32[]{:S(2)}, u32[]{:S(2)}) %collective-permute-start.5) | collective-permute-done | bytes 131104 | tf_op jit(solution)/shard_map/ppermute | solution.py:59
  53.0 0.7 copy-done.14
  53.7 7.1 %collective-permute-done.6 = bf16[128,512]{1,0:T(8,128)(2,1)S(1)} collective-permute-done((bf16[128,512]{1,0:T(8,128)(2,1)S(1)}, bf16[128,512]{1,0:T(8,128)(2,1)S(1)}, u32[]{:S(2)}, u32[]{:S(2)}) %collective-permute-start.6) | collective-permute-done | bytes 131104 | tf_op jit(solution)/shard_map/ppermute | solution.py:59
  60.7 0.7 copy-done.16
  61.4 7.1 %collective-permute-done.7 = bf16[128,512]{1,0:T(8,128)(2,1)S(1)} collective-permute-done((bf16[128,512]{1,0:T(8,128)(2,1)S(1)}, bf16[128,512]{1,0:T(8,128)(2,1)S(1)}, u32[]{:S(2)}, u32[]{:S(2)}) %collective-permute-start.7) | collective-permute-done | bytes 131104 | tf_op jit(solution)/shard_map/ppermute | solution.py:59
  68.5 0.7 copy-done.18
  69.1 7.1 %collective-permute-done.8 = bf16[128,512]{1,0:T(8,128)(2,1)S(1)} collective-permute-done((bf16[128,512]{1,0:T(8,128)(2,1)S(1)}, bf16[128,512]{1,0:T(8,128)(2,1)S(1)}, u32[]{:S(2)}, u32[]{:S(2)}) %collective-permute-start.8) | collective-permute-done | bytes 131104 | tf_op jit(solution)/shard_map/ppermute | solution.py:59
  76.2 0.7 copy-done.20
  76.9 7.2 %collective-permute-done.9 = bf16[128,512]{1,0:T(8,128)(2,1)} collective-permute-done((bf16[128,512]{1,0:T(8,128)(2,1)S(1)}, bf16[128,512]{1,0:T(8,128)(2,1)}, u32[]{:S(2)}, u32[]{:S(2)}) %collective-permute-start.9) | collective-permute-done | bytes 131104 | tf_op jit(solution)/shard_map/ppermute | solution.py:59
  84.1 8.8 %multiply_reduce_fusion.1 = f32[1024]{0:T(1024)S(1)} fusion(bf16[8192,1024]{1,0:T(8,128)(2,1)} %param.9, bf16[8192,128]{1,0:T(8,128)(2,1)} %param.11, bf16[2,64,1024]{2,1,0:T(8,128)(2,1)} %param.12), kind=kOutput, calls=%fused_computation.1 | convolution fusion | flops 1107295232 | bytes 19009536 | tf_op jit(solution)/shard_map/dot_general | solution.py:47
  93.0 5.4 %multiply_reduce_fusion = f32[1024]{0:T(1024)S(1)} fusion(bf16[8192,1024]{1,0:T(8,128)(2,1)S(1)} %copy-done, bf16[8192,128]{1,0:T(8,128)(2,1)S(1)} %copy-done.3, bf16[2,64,1024]{2,1,0:T(8,128)(2,1)S(1)} %copy-done.5), kind=kOutput, calls=%fused_computation | convolution fusion | flops 1107295232 | bytes 19009536 | tf_op jit(solution)/shard_map/dot_general | solution.py:47
  98.5 1.9 collective-permute-done.11
  100.4 7.3 %collective-permute-done.12 = bf16[128,512]{1,0:T(8,128)(2,1)S(1)} collective-permute-done((bf16[128,512]{1,0:T(8,128)(2,1)}, bf16[128,512]{1,0:T(8,128)(2,1)S(1)}, u32[]{:S(2)}, u32[]{:S(2)}) %collective-permute-start.12) | collective-permute-done | bytes 131104 | tf_op jit(solution)/shard_map/ppermute | solution.py:59
  107.7 7.1 %collective-permute-done.13 = bf16[128,512]{1,0:T(8,128)(2,1)S(1)} collective-permute-done((bf16[128,512]{1,0:T(8,128)(2,1)S(1)}, bf16[128,512]{1,0:T(8,128)(2,1)S(1)}, u32[]{:S(2)}, u32[]{:S(2)}) %collective-permute-start.13) | collective-permute-done | bytes 131104 | tf_op jit(solution)/shard_map/ppermute | solution.py:59
  114.8 7.1 %collective-permute-done.14 = bf16[128,512]{1,0:T(8,128)(2,1)S(1)} collective-permute-done((bf16[128,512]{1,0:T(8,128)(2,1)S(1)}, bf16[128,512]{1,0:T(8,128)(2,1)S(1)}, u32[]{:S(2)}, u32[]{:S(2)}) %collective-permute-start.14) | collective-permute-done | bytes 131104 | tf_op jit(solution)/shard_map/ppermute | solution.py:59
  121.9 0.9 constant_dynamic-update-slice_fusion.28
  122.8 0.9 constant_dynamic-update-slice_fusion.27
  123.8 0.9 constant_dynamic-update-slice_fusion.26
  124.7 0.9 constant_dynamic-update-slice_fusion.25
  125.6 0.9 constant_dynamic-update-slice_fusion.24
  126.5 0.9 constant_dynamic-update-slice_fusion.23
  127.4 0.9 constant_dynamic-update-slice_fusion.22
  128.3 0.9 constant_dynamic-update-slice_fusion.21
  129.3 0.9 constant_dynamic-update-slice_fusion.20
  130.2 0.9 constant_dynamic-update-slice_fusion.19
  131.1 0.9 constant_dynamic-update-slice_fusion.18
  132.1 0.9 constant_dynamic-update-slice_fusion.12
  133.0 0.9 constant_dynamic-update-slice_fusion.11
  134.0 0.9 constant_dynamic-update-slice_fusion.10
  135.2 1.0 convolution_convert_fusion
  136.2 0.2 fusion.21
  136.4 0.2 fusion.26
  136.7 9.4 %convolution_add_fusion.2 = f32[128,1024]{1,0:T(8,128)S(1)} fusion(f32[128,1024]{1,0:T(8,128)S(1)} %fusion.21, bf16[8192,1024]{1,0:T(8,128)(2,1)} %param.10, bf16[128,16384]{1,0:T(8,128)(2,1)S(1)} %constant_dynamic-update-slice_fusion, s32[]{:T(128)S(6)} %select_n.17), kind=kOutput, calls=%fused_computation.7 | convolution fusion | flops 2147614720 | bytes 19922948 | tf_op jit(solution)/shard_map/dot_general | solution.py:65
  146.1 1.2 slice-done.3
  147.3 3.6 %multiply_reduce_fusion.3 = (f32[1024]{0:T(1024)S(1)}, f32[1024]{0:T(1024)S(1)}, bf16[128,1024]{1,0:T(8,128)(2,1)S(1)}, bf16[128,1024]{1,0:T(8,128)(2,1)}, bf16[128,1024]{1,0:T(8,128)(2,1)S(1)}) fusion(f32[1024]{0:T(1024)S(1)} %bitcast.53, f32[128,1024]{1,0:T(8,128)S(1)} %convolution_add_fusion.2, f32[1024]{0:T(1024)S(1)} %bitcast.54, ...), kind=kOutput, calls=%fused_computation.32 | convolution fusion | flops 2150889472 | bytes 20987908 | tf_op jit(solution)/shard_map/dot_general | solution.py:64
  151.0 0.2 fusion.23
  151.2 13.3 %fusion.48 = f32[128,8192]{1,0:T(8,128)} fusion(bf16[128,1024]{1,0:T(8,128)(2,1)S(1)} %get-tuple-element.14, bf16[8192,1024]{1,0:T(8,128)(2,1)} %param.9), kind=kOutput, calls=%fused_computation.110 | convolution fusion | flops 2147483648 | bytes 21233664 | tf_op jit(solution)/shard_map/dot_general | solution.py:22
  164.5 0.2 fusion.18
  164.7 0.6 pad_maximum_fusion.1
  165.4 0.3 reduce-scatter.2.cloned.1.call-start
  165.7 14.6 %convolution_add_fusion.1 = f32[128,8192]{1,0:T(8,128)} fusion(f32[128,8192]{1,0:T(8,128)} %fusion.48, bf16[128,1024]{1,0:T(8,128)(2,1)S(1)} %get-tuple-element.16, bf16[8192,1024]{1,0:T(8,128)(2,1)} %param.10), kind=kOutput, calls=%fused_computation.4 | convolution fusion | flops 2148532224 | bytes 25427968 | tf_op jit(solution)/shard_map/dot_general | solution.py:22
  180.3 0.6 multiply_reduce_fusion.5
  181.3 0.7 multiply_reduce_fusion.4
  183.3 30.0 %psum.15 = f32[]{:T(128)} all-reduce(f32[]{:T(128)S(6)} %add.111), channel_id=1, replica_groups=mesh['groups'=2,'out'=16] {'out'}, use_global_device_ids=true, to_apply=%region_8.9 | all-reduce | flops 1 | bytes 8 | tf_op jit(solution)/shard_map/psum | solution.py:100
  213.3 34.4 %all-reduce.2.cloned.1.call-done = f32[128,128]{0,1:T(8,128)} async-done(((f32[128,128]{0,1:T(8,128)}), f32[128,128]{0,1:T(8,128)}) %all-reduce.2.cloned.1.call-update) | async-done | bytes 65552 | tf_op jit(solution)/shard_map/psum | solution.py:100
  247.7 0.9 subtract_convert_fusion
  248.7 2.5 fusion.8
  251.2 0.3 copy-done.2
  251.5 1.9 fusion.3
  255.1 0.8 copy.12
  255.9 0.6 broadcast_divide_fusion
  256.5 0.9 fusion.17
  257.4 0.2 fusion.29
  257.6 68.8 %reduce-scatter.2.cloned.1.call-done = f32[128,512]{1,0:T(8,128)} async-done(((f32[128,8192]{1,0:T(8,128)}), f32[128,512]{1,0:T(8,128)}) %reduce-scatter.2.cloned.1.call-update) | async-done | bytes 262160 | tf_op jit(solution)/shard_map/reduce_scatter | solution.py:98
  326.3 1.8 fusion.7
  (93 shorter events, 1.2 us)
Async XLA Ops:
  7.2 85.8 %copy-start.3 = (bf16[8192,128]{1,0:T(8,128)(2,1)S(1)}, bf16[8192,128]{1,0:T(8,128)(2,1)}, u32[]{:S(2)}) copy-start(bf16[8192,128]{1,0:T(8,128)(2,1)} %param.11) | copy-start | bytes 6291460
  7.2 85.8 %copy-start.5 = (bf16[2,64,1024]{2,1,0:T(8,128)(2,1)S(1)}, bf16[2,64,1024]{2,1,0:T(8,128)(2,1)}, u32[]{:S(2)}) copy-start(bf16[2,64,1024]{2,1,0:T(8,128)(2,1)} %param.12) | copy-start | bytes 786436
  7.2 240.5 %all-reduce.2.cloned.1.call-start = ((), (), s32[]{:S(2)}) async-start(), calls=%async_computation.2 | async-start | bytes 131072 | tf_op jit(solution)/shard_map/psum | solution.py:100
  7.2 85.8 %copy-start = (bf16[8192,1024]{1,0:T(8,128)(2,1)S(1)}, bf16[8192,1024]{1,0:T(8,128)(2,1)}, u32[]{:S(2)}) copy-start(bf16[8192,1024]{1,0:T(8,128)(2,1)} %param.10) | copy-start | bytes 50331652
  7.2 8.4 %collective-permute-start = (bf16[128,512]{1,0:T(8,128)(2,1)}, bf16[128,512]{1,0:T(8,128)(2,1)S(1)}, u32[]{:S(2)}, u32[]{:S(2)}) collective-permute-start(bf16[128,512]{1,0:T(8,128)(2,1)} %param.7), channel_id=1, source_target_pairs={{0,1},{1,2},{2,3},{3,4},{4,5},{5,6},{6,7},{7,8},{8,9},{9,10},{10,1... | collective-permute-start | bytes 393224 | tf_op jit(solution)/shard_map/ppermute | solution.py:59
  15.6 7.1 %collective-permute-start.1 = (bf16[128,512]{1,0:T(8,128)(2,1)S(1)}, bf16[128,512]{1,0:T(8,128)(2,1)S(1)}, u32[]{:S(2)}, u32[]{:S(2)}) collective-permute-start(bf16[128,512]{1,0:T(8,128)(2,1)S(1)} %collective-permute-done), channel_id=1, source_target_pairs={{0,1},{1,2},{2,3},{3,4},{4,5},{5,6},{6,7},{7,8},{8,9},{9,10},{10,1... | collective-permute-start | bytes 393224 | tf_op jit(solution)/shard_map/ppermute | solution.py:59
  22.7 61.4 %copy-start.6 = (bf16[128,512]{1,0:T(8,128)(2,1)}, bf16[128,512]{1,0:T(8,128)(2,1)S(1)}, u32[]{:S(2)}) copy-start(bf16[128,512]{1,0:T(8,128)(2,1)S(1)} %collective-permute-done.1) | copy-start | bytes 393220
  22.7 7.1 %collective-permute-start.2 = (bf16[128,512]{1,0:T(8,128)(2,1)S(1)}, bf16[128,512]{1,0:T(8,128)(2,1)S(1)}, u32[]{:S(2)}, u32[]{:S(2)}) collective-permute-start(bf16[128,512]{1,0:T(8,128)(2,1)S(1)} %collective-permute-done.1), channel_id=1, source_target_pairs={{0,1},{1,2},{2,3},{3,4},{4,5},{5,6},{6,7},{7,8},{8,9},{9,10},{10,1... | collective-permute-start | bytes 393224 | tf_op jit(solution)/shard_map/ppermute | solution.py:59
  29.8 0.6 copy-start.8
  30.4 7.1 %collective-permute-start.3 = (bf16[128,512]{1,0:T(8,128)(2,1)S(1)}, bf16[128,512]{1,0:T(8,128)(2,1)S(1)}, u32[]{:S(2)}, u32[]{:S(2)}) collective-permute-start(bf16[128,512]{1,0:T(8,128)(2,1)S(1)} %collective-permute-done.2), channel_id=1, source_target_pairs={{0,1},{1,2},{2,3},{3,4},{4,5},{5,6},{6,7},{7,8},{8,9},{9,10},{10,1... | collective-permute-start | bytes 393224 | tf_op jit(solution)/shard_map/ppermute | solution.py:59
  37.5 0.6 copy-start.10
  38.2 7.1 %collective-permute-start.4 = (bf16[128,512]{1,0:T(8,128)(2,1)S(1)}, bf16[128,512]{1,0:T(8,128)(2,1)S(1)}, u32[]{:S(2)}, u32[]{:S(2)}) collective-permute-start(bf16[128,512]{1,0:T(8,128)(2,1)S(1)} %collective-permute-done.3), channel_id=1, source_target_pairs={{0,1},{1,2},{2,3},{3,4},{4,5},{5,6},{6,7},{7,8},{8,9},{9,10},{10,1... | collective-permute-start | bytes 393224 | tf_op jit(solution)/shard_map/ppermute | solution.py:59
  45.3 0.6 copy-start.12
  45.9 7.1 %collective-permute-start.5 = (bf16[128,512]{1,0:T(8,128)(2,1)S(1)}, bf16[128,512]{1,0:T(8,128)(2,1)S(1)}, u32[]{:S(2)}, u32[]{:S(2)}) collective-permute-start(bf16[128,512]{1,0:T(8,128)(2,1)S(1)} %collective-permute-done.4), channel_id=1, source_target_pairs={{0,1},{1,2},{2,3},{3,4},{4,5},{5,6},{6,7},{7,8},{8,9},{9,10},{10,1... | collective-permute-start | bytes 393224 | tf_op jit(solution)/shard_map/ppermute | solution.py:59
  53.0 0.7 copy-start.14
  53.7 7.1 %collective-permute-start.6 = (bf16[128,512]{1,0:T(8,128)(2,1)S(1)}, bf16[128,512]{1,0:T(8,128)(2,1)S(1)}, u32[]{:S(2)}, u32[]{:S(2)}) collective-permute-start(bf16[128,512]{1,0:T(8,128)(2,1)S(1)} %collective-permute-done.5), channel_id=1, source_target_pairs={{0,1},{1,2},{2,3},{3,4},{4,5},{5,6},{6,7},{7,8},{8,9},{9,10},{10,1... | collective-permute-start | bytes 393224 | tf_op jit(solution)/shard_map/ppermute | solution.py:59
  60.7 0.7 copy-start.16
  61.4 7.1 %collective-permute-start.7 = (bf16[128,512]{1,0:T(8,128)(2,1)S(1)}, bf16[128,512]{1,0:T(8,128)(2,1)S(1)}, u32[]{:S(2)}, u32[]{:S(2)}) collective-permute-start(bf16[128,512]{1,0:T(8,128)(2,1)S(1)} %collective-permute-done.6), channel_id=1, source_target_pairs={{0,1},{1,2},{2,3},{3,4},{4,5},{5,6},{6,7},{7,8},{8,9},{9,10},{10,1... | collective-permute-start | bytes 393224 | tf_op jit(solution)/shard_map/ppermute | solution.py:59
  68.5 0.7 copy-start.18
  69.1 7.1 %collective-permute-start.8 = (bf16[128,512]{1,0:T(8,128)(2,1)S(1)}, bf16[128,512]{1,0:T(8,128)(2,1)S(1)}, u32[]{:S(2)}, u32[]{:S(2)}) collective-permute-start(bf16[128,512]{1,0:T(8,128)(2,1)S(1)} %collective-permute-done.7), channel_id=1, source_target_pairs={{0,1},{1,2},{2,3},{3,4},{4,5},{5,6},{6,7},{7,8},{8,9},{9,10},{10,1... | collective-permute-start | bytes 393224 | tf_op jit(solution)/shard_map/ppermute | solution.py:59
  76.2 0.7 copy-start.20
  76.9 7.2 %collective-permute-start.9 = (bf16[128,512]{1,0:T(8,128)(2,1)S(1)}, bf16[128,512]{1,0:T(8,128)(2,1)}, u32[]{:S(2)}, u32[]{:S(2)}) collective-permute-start(bf16[128,512]{1,0:T(8,128)(2,1)S(1)} %collective-permute-done.8), channel_id=1, source_target_pairs={{0,1},{1,2},{2,3},{3,4},{4,5},{5,6},{6,7},{7,8},{8,9},{9,10},{10,1... | collective-permute-start | bytes 393224 | tf_op jit(solution)/shard_map/ppermute | solution.py:59
  84.1 8.8 %collective-permute-start.10 = (bf16[128,512]{1,0:T(8,128)(2,1)}, bf16[128,512]{1,0:T(8,128)(2,1)}, u32[]{:S(2)}, u32[]{:S(2)}) collective-permute-start(bf16[128,512]{1,0:T(8,128)(2,1)} %collective-permute-done.9), channel_id=1, source_target_pairs={{0,1},{1,2},{2,3},{3,4},{4,5},{5,6},{6,7},{7,8},{8,9},{9,10},{10,1... | collective-permute-start | bytes 393224 | tf_op jit(solution)/shard_map/ppermute | solution.py:59
  92.9 21.9 %copy-start.22 = (f32[2,1024]{1,0:T(2,128)S(1)}, f32[2,1024]{1,0:T(2,128)}, u32[]{:S(2)}) copy-start(f32[2,1024]{1,0:T(2,128)} %param.13) | copy-start | bytes 24580
  92.9 39.1 %copy-start.4 = (bf16[128,512]{1,0:T(8,128)(2,1)S(1)}, bf16[128,512]{1,0:T(8,128)(2,1)}, u32[]{:S(2)}) copy-start(bf16[128,512]{1,0:T(8,128)(2,1)} %param.7) | copy-start | bytes 393220
  92.9 7.5 %collective-permute-start.11 = (bf16[128,512]{1,0:T(8,128)(2,1)}, bf16[128,512]{1,0:T(8,128)(2,1)}, u32[]{:S(2)}, u32[]{:S(2)}) collective-permute-start(bf16[128,512]{1,0:T(8,128)(2,1)} %collective-permute-done.10), channel_id=1, source_target_pairs={{0,1},{1,2},{2,3},{3,4},{4,5},{5,6},{6,7},{7,8},{8,9},{9,10},{10,1... | collective-permute-start | bytes 393224 | tf_op jit(solution)/shard_map/ppermute | solution.py:59
  98.4 36.5 %copy-start.17 = (bf16[128,512]{1,0:T(8,128)(2,1)S(1)}, bf16[128,512]{1,0:T(8,128)(2,1)}, u32[]{:S(2)}) copy-start(bf16[128,512]{1,0:T(8,128)(2,1)} %copy-done.16) | copy-start | bytes 393220
  98.4 36.5 %copy-start.15 = (bf16[128,512]{1,0:T(8,128)(2,1)S(1)}, bf16[128,512]{1,0:T(8,128)(2,1)}, u32[]{:S(2)}) copy-start(bf16[128,512]{1,0:T(8,128)(2,1)} %copy-done.14) | copy-start | bytes 393220
  98.4 36.6 %copy-start.13 = (bf16[128,512]{1,0:T(8,128)(2,1)S(1)}, bf16[128,512]{1,0:T(8,128)(2,1)}, u32[]{:S(2)}) copy-start(bf16[128,512]{1,0:T(8,128)(2,1)} %copy-done.12) | copy-start | bytes 393220
  98.4 36.6 %copy-start.11 = (bf16[128,512]{1,0:T(8,128)(2,1)S(1)}, bf16[128,512]{1,0:T(8,128)(2,1)}, u32[]{:S(2)}) copy-start(bf16[128,512]{1,0:T(8,128)(2,1)} %copy-done.10) | copy-start | bytes 393220
  98.5 36.6 %copy-start.9 = (bf16[128,512]{1,0:T(8,128)(2,1)S(1)}, bf16[128,512]{1,0:T(8,128)(2,1)}, u32[]{:S(2)}) copy-start(bf16[128,512]{1,0:T(8,128)(2,1)} %copy-done.8) | copy-start | bytes 393220
  98.5 36.6 %copy-start.7 = (bf16[128,512]{1,0:T(8,128)(2,1)S(1)}, bf16[128,512]{1,0:T(8,128)(2,1)}, u32[]{:S(2)}) copy-start(bf16[128,512]{1,0:T(8,128)(2,1)} %copy-done.6) | copy-start | bytes 393220
  98.5 36.4 %copy-start.21 = (bf16[128,512]{1,0:T(8,128)(2,1)S(1)}, bf16[128,512]{1,0:T(8,128)(2,1)}, u32[]{:S(2)}) copy-start(bf16[128,512]{1,0:T(8,128)(2,1)} %copy-done.20) | copy-start | bytes 393220
  98.5 36.4 %copy-start.19 = (bf16[128,512]{1,0:T(8,128)(2,1)S(1)}, bf16[128,512]{1,0:T(8,128)(2,1)}, u32[]{:S(2)}) copy-start(bf16[128,512]{1,0:T(8,128)(2,1)} %copy-done.18) | copy-start | bytes 393220
  100.4 7.3 %collective-permute-start.12 = (bf16[128,512]{1,0:T(8,128)(2,1)}, bf16[128,512]{1,0:T(8,128)(2,1)S(1)}, u32[]{:S(2)}, u32[]{:S(2)}) collective-permute-start(bf16[128,512]{1,0:T(8,128)(2,1)} %collective-permute-done.11), channel_id=1, source_target_pairs={{0,1},{1,2},{2,3},{3,4},{4,5},{5,6},{6,7},{7,8},{8,9},{9,10},{10,1... | collective-permute-start | bytes 393224 | tf_op jit(solution)/shard_map/ppermute | solution.py:59
  107.7 7.1 %collective-permute-start.13 = (bf16[128,512]{1,0:T(8,128)(2,1)S(1)}, bf16[128,512]{1,0:T(8,128)(2,1)S(1)}, u32[]{:S(2)}, u32[]{:S(2)}) collective-permute-start(bf16[128,512]{1,0:T(8,128)(2,1)S(1)} %collective-permute-done.12), channel_id=1, source_target_pairs={{0,1},{1,2},{2,3},{3,4},{4,5},{5,6},{6,7},{7,8},{8,9},{9,10},{10,1... | collective-permute-start | bytes 393224 | tf_op jit(solution)/shard_map/ppermute | solution.py:59
  114.8 7.1 %collective-permute-start.14 = (bf16[128,512]{1,0:T(8,128)(2,1)S(1)}, bf16[128,512]{1,0:T(8,128)(2,1)S(1)}, u32[]{:S(2)}, u32[]{:S(2)}) collective-permute-start(bf16[128,512]{1,0:T(8,128)(2,1)S(1)} %collective-permute-done.13), channel_id=1, source_target_pairs={{0,1},{1,2},{2,3},{3,4},{4,5},{5,6},{6,7},{7,8},{8,9},{9,10},{10,1... | collective-permute-start | bytes 393224 | tf_op jit(solution)/shard_map/ppermute | solution.py:59
  135.1 10.9 %copy-start.1 = (bf16[128,16384]{1,0:T(8,128)(2,1)}, bf16[128,16384]{1,0:T(8,128)(2,1)S(1)}, u32[]{:S(2)}) copy-start(bf16[128,16384]{1,0:T(8,128)(2,1)S(1)} %constant_dynamic-update-slice_fusion) | copy-start | bytes 12582916
  135.2 10.9 %slice-start = ((s8[16777216]{0:T(1024)(128)(4,1)}), s8[4194304]{0:T(1024)(128)(4,1)S(1)}, s32[]{:S(2)}) async-start(s8[16777216]{0:T(1024)(128)(4,1)} %bitcast.45), calls=%async_computation.3 | async-start | bytes 8388608
  136.7 9.4 %slice-start.1 = ((s8[16777216]{0:T(1024)(128)(4,1)}), s8[4194304]{0:T(1024)(128)(4,1)S(1)}, s32[]{:S(2)}) async-start(s8[16777216]{0:T(1024)(128)(4,1)} %bitcast.45), calls=%async_computation.4 | async-start | bytes 8388608
  136.7 9.4 %slice-start.2 = ((s8[16777216]{0:T(1024)(128)(4,1)}), s8[4194304]{0:T(1024)(128)(4,1)S(1)}, s32[]{:S(2)}) async-start(s8[16777216]{0:T(1024)(128)(4,1)} %bitcast.45), calls=%async_computation.5 | async-start | bytes 8388608
  136.7 10.6 %slice-start.3 = ((s8[16777216]{0:T(1024)(128)(4,1)}), s8[4194304]{0:T(1024)(128)(4,1)S(1)}, s32[]{:S(2)}) async-start(s8[16777216]{0:T(1024)(128)(4,1)} %bitcast.45), calls=%async_computation.6 | async-start | bytes 8388608
  136.7 10.6 %copy-start.23 = (bf16[128,1024]{1,0:T(8,128)(2,1)S(1)}, bf16[128,1024]{1,0:T(8,128)(2,1)}, u32[]{:S(2)}) copy-start(bf16[128,1024]{1,0:T(8,128)(2,1)} %param.8) | copy-start | bytes 786436
  165.4 161.0 %reduce-scatter.2.cloned.1.call-start = ((), (), s32[]{:S(2)}) async-start(), calls=%async_computation.1 | async-start | bytes 4456448 | tf_op jit(solution)/shard_map/reduce_scatter | solution.py:98
  248.7 2.8 copy-start.2
Sparse Core Ops, SparseCore 0:
  165.5 82.1 all-reduce.1
  252.1 74.2 reduce-scatter.1
